TPU v7x, 32 devices: a whole 2x2x4 slice. The times are simulated.
32 devices in a mesh: slab: 4 (over y, x), leaf: 8 (over z, core).
Axes of the slice: x: 2, y: 2, z: 4, core: 2. Of those that a mesh axis runs over, the one named last changes fastest.
Arguments:
- right_sides: bfloat16 [32, 131072], P(None, ('slab', 'leaf')), may hold values from -6 to 6
- left_sides: bfloat16 [32, 131072], P(None, ('slab', 'leaf')), may hold values from -6 to 6
- near_blocks: bfloat16 [1024, 8, 128, 128], P(('slab', 'leaf')), may hold values from -0.1875 to 0.1875
- near_columns: int32 [1024, 8], P(('slab', 'leaf')), may hold values from 0 to 1023, as said below
- cluster_points: int32 [1024], P(('slab', 'leaf')), may hold values from 64 to 128, as said below
- leaf_basis: bfloat16 [1024, 64, 128], P(('slab', 'leaf')), may hold values from -0.5 to 0.5
- transfer: float32 [1024, 64, 128], P(('slab', 'leaf')), may hold values from -0.625 to 0.625
- far_parents: int32 [32, 24], P(('slab', 'leaf')), may hold values from 0 to 31, as said below
- far_count: int32 [32], P(('slab', 'leaf')), may hold values from 12 to 24, as said below
- coupling: float32 [32, 24, 128, 128], P(('slab', 'leaf')), may hold values from -0.375 to 0.375
- slab_transfer: float32 [32, 128, 128], P(('slab', 'leaf')), may hold values from -0.75 to 0.75
- apex_coupling: float32 [4, 4, 128, 128], replicated, may hold values from -0.75 to 0.75
Outputs:
- product: float32 [32, 131072], P(None, ('slab', 'leaf'))
- adjoint_product: float32 [32, 131072], P(None, ('slab', 'leaf'))
Inputs may be any that keep to these rules, and one draw needn't show every extreme that they name: `near_columns`: row i holds 8 different clusters, i among them, all inside the window of 9 consecutive clusters centred on i, moved inward where it would pass an end of 0 to 1023. `cluster_points`: some cluster has exactly 128 points and some exactly 64. `far_parents`: row p holds 24 different parents, none equal to p; only the first far_count[p] are used. `far_count`: some parent uses all 24 slots and some exactly 12.
All inputs are finite; a program needn't handle non-finite values.
Results may differ from a plain program's by a relative error of at most 0.0024.
Values may be sent and summed in bfloat16 or wider, within the bound.
A program may use at most 128 MiB of HBM per device.

v0:
```python
import jax
import jax.numpy as jnp
from jax import lax
from jax.sharding import PartitionSpec as P

B = 128
HW = 4


def extended_2(value, sides, width):
    for axis, dim in sides:
        size, length = (lax.axis_size(axis), value.shape[dim])
        up = [(i, (i + 1) % size) for i in range(size - 1)]
        down = [(j, i) for i, j in up]
        last = lax.slice_in_dim(value, length - width, length, axis=dim)
        first = lax.slice_in_dim(value, 0, width, axis=dim)
        before = lax.ppermute(last, axis, up)
        after = lax.ppermute(first, axis, down)
        value = jnp.concatenate([before, value, after], axis=dim)
    return value


def passed_along(block, axis, distance):
    devices = range(lax.axis_size(axis))
    route = [(i - distance, i) for i in devices if i - distance in devices]
    return lax.ppermute(block, axis, route)


def shards(
    right_sides,
    left_sides,
    near_blocks,
    near_columns,
    cluster_points,
    leaf_basis,
    transfer,
    far_parents,
    far_count,
    coupling,
    slab_transfer,
    apex_coupling,
):
    uppermost_level = lax.Precision.HIGHEST
    rhs_count = right_sides.shape[0]
    clusters = near_blocks.shape[0]
    device = lax.axis_index(("slab", "leaf"))
    devices_all = lax.axis_size(("slab", "leaf"))
    slab_index = lax.axis_index("slab")
    slab_count = lax.axis_size("slab")
    point_mask = jnp.arange(B, dtype=jnp.int32)[None, :] < cluster_points[:, None]
    zero_bf = jnp.zeros((), jnp.bfloat16)
    masked_right = jnp.where(point_mask[None], right_sides.reshape(rhs_count, clusters, B), zero_bf)
    masked_left = jnp.where(point_mask[None], left_sides.reshape(rhs_count, clusters, B), zero_bf)
    extended = extended_2(
        masked_right.reshape(rhs_count, clusters * B), ((("slab", "leaf"), 1),), HW * B
    )
    extended = extended.reshape(rhs_count, clusters + 2 * HW, B)
    offsets = near_columns - (device * clusters - HW)
    picked = jnp.take(extended, offsets, axis=1)
    near_out = jnp.einsum("csab,rcsb->rca", near_blocks, picked, preferred_element_type=jnp.float32)
    contrib = jnp.einsum(
        "csab,rca->csrb", near_blocks, masked_left, preferred_element_type=jnp.float32
    )
    collected = jax.ops.segment_sum(
        contrib.reshape(-1, rhs_count, B), offsets.reshape(-1), num_segments=clusters + 2 * HW
    )
    from_next = passed_along(collected[:HW].astype(jnp.bfloat16), ("slab", "leaf"), -1).astype(
        jnp.float32
    )
    from_prev = passed_along(
        collected[clusters + HW :].astype(jnp.bfloat16), ("slab", "leaf"), 1
    ).astype(jnp.float32)
    middle = collected[HW : clusters + HW]
    middle = middle.at[clusters - HW :].add(from_next).at[:HW].add(from_prev)
    near_back = jnp.transpose(middle, (1, 0, 2))
    leaf_right = jnp.einsum(
        "ckb,rcb->ckr", leaf_basis, masked_right, preferred_element_type=jnp.float32
    )
    leaf_left = jnp.einsum(
        "ckb,rcb->ckr", leaf_basis, masked_left, preferred_element_type=jnp.float32
    )
    parent_right = jnp.einsum("ckq,ckr->qr", transfer, leaf_right, precision=uppermost_level)
    parent_left = jnp.einsum("ckq,ckr->qr", transfer, leaf_left, precision=uppermost_level)
    targets = far_parents[0]
    live_slots = jnp.arange(targets.shape[0], dtype=jnp.int32) < far_count[0]
    couple = coupling[0]
    piece = lax.all_gather(parent_right[None], ("slab", "leaf"), axis=0, tiled=True)
    owners = jnp.arange(piece.shape[0], dtype=jnp.int32)
    select = ((targets[:, None] == owners[None, :]) & live_slots[:, None]).astype(jnp.float32)
    chosen = jnp.einsum("fn,nqr->fqr", select, piece, precision=uppermost_level)
    far_right = jnp.einsum("fab,fbr->ar", couple, chosen, precision=uppermost_level)
    outward = jnp.einsum("fab,ar->fbr", couple, parent_left, precision=uppermost_level)
    routing = (
        (targets[:, None] == jnp.arange(devices_all, dtype=jnp.int32)[None, :])
        & live_slots[:, None]
    ).astype(jnp.float32)
    spread = jnp.einsum("fp,fbr->pbr", routing, outward, precision=uppermost_level)
    arrived = lax.all_to_all(spread, ("slab", "leaf"), split_axis=0, concat_axis=0, tiled=True)
    far_left = jnp.sum(arrived, axis=0)
    lift = slab_transfer[0]
    slab_share = jnp.stack(
        [
            jnp.einsum("qt,qr->tr", lift, parent_right, precision=uppermost_level),
            jnp.einsum("qt,qr->tr", lift, parent_left, precision=uppermost_level),
        ]
    )
    within = lax.psum(slab_share, "leaf")
    slab_sum_totals = lax.all_gather(within[None], "slab", axis=0, tiled=True)
    remaining_slabs = (jnp.arange(slab_count, dtype=jnp.int32) != slab_index).astype(jnp.float32)
    row_block_list = lax.dynamic_index_in_dim(apex_coupling, slab_index, 0, keepdims=False)
    column_blocks = lax.dynamic_index_in_dim(apex_coupling, slab_index, 1, keepdims=False)
    apex_right = jnp.einsum(
        "j,jiv,jvq->iq",
        remaining_slabs,
        row_block_list,
        slab_sum_totals[:, 0],
        precision=uppermost_level,
    )
    apex_left = jnp.einsum(
        "s,sab,sar->br",
        remaining_slabs,
        column_blocks,
        slab_sum_totals[:, 1],
        precision=uppermost_level,
    )
    hat_right = far_right + jnp.einsum("qt,tr->qr", lift, apex_right, precision=uppermost_level)
    hat_left = far_left + jnp.einsum("qt,tr->qr", lift, apex_left, precision=uppermost_level)
    down_right = jnp.einsum("ckq,qr->ckr", transfer, hat_right, precision=uppermost_level).astype(
        jnp.bfloat16
    )
    down_left = jnp.einsum("ckq,qr->ckr", transfer, hat_left, precision=uppermost_level).astype(
        jnp.bfloat16
    )
    far_out = jnp.einsum("ckb,ckr->rcb", leaf_basis, down_right, preferred_element_type=jnp.float32)
    far_back = jnp.einsum("ckb,ckr->rcb", leaf_basis, down_left, preferred_element_type=jnp.float32)
    zero_wide = jnp.zeros((), jnp.float32)
    product = jnp.where(point_mask[None], near_out + far_out, zero_wide).reshape(
        rhs_count, clusters * B
    )
    adjoint_product = jnp.where(point_mask[None], near_back + far_back, zero_wide).reshape(
        rhs_count, clusters * B
    )
    return (product, adjoint_product)


def solution(mesh):
    return jax.shard_map(
        shards,
        mesh=mesh,
        in_specs=(
            P(None, ("slab", "leaf")),
            P(None, ("slab", "leaf")),
            P(("slab", "leaf"), None, None, None),
            P(("slab", "leaf"), None),
            P(("slab", "leaf")),
            P(("slab", "leaf"), None, None),
            P(("slab", "leaf"), None, None),
            P(("slab", "leaf"), None),
            P(("slab", "leaf")),
            P(("slab", "leaf"), None, None, None),
            P(("slab", "leaf"), None, None),
            P(),
        ),
        out_specs=(P(None, ("slab", "leaf")), P(None, ("slab", "leaf"))),
        check_vma=False,
    )
```

profile of v0, /device:TPU:9, one launch (start us, length us, event | category | flops | bytes accessed | tf_op | source)
XLA Modules:
  0.0 177.3 jit_solution(13958339036343607816)
XLA Ops:
  0.6 0.0 copy-start
  0.7 0.8 compare_and_fusion
  1.5 0.1 copy.46
  1.5 0.1 reshape.132
  1.6 0.7 iota_compare_fusion
  2.4 6.7 %fusion.31 = f32[32,32,8,128]{3,1,2,0:T(8,128)} fusion(bf16[32,8,128,128]{3,2,1,0:T(8,128)(2,1)} %param.18, pred[32,128]{1,0:T(8,128)(4,1)S(1)} %iota_compare_fusion, bf16[32,4096]{1,0:T(8,128)(2,1)} %param.17), kind=kOutput, calls=%fused_computation.45 | convolution fusion | flops 268566528 | bytes 12849152 | tf_op jit(solution)/shard_map/csab,rca->csrb/dot_general | solution.py:61
  9.0 0.1 broadcast_in_dim.78
  9.1 0.0 copy-start.4
  9.1 22.6 %scatter_fusion = f32[40,32,128]{2,1,0:T(8,128)S(1)} fusion(f32[40,32,128]{2,1,0:T(8,128)S(1)} %broadcast_in_dim.78, s32[256]{0:T(256)S(1)} %reshape.132, f32[256,32,128]{2,1,0:T(8,128)} %bitcast.168), kind=kCustom, calls=%fused_computation.1 | custom fusion | flops 1048576 | bytes 12583936 | tf_op jit(solution)/shard_map/scatter-add | solution.py:64
  31.7 0.0 copy-start.1
  31.7 0.1 convert.9
  31.8 0.6 fusion.70
  32.4 2.6 %collective-permute-start.2 = (bf16[4,32,128]{2,1,0:T(8,128)(2,1)}, bf16[4,32,128]{2,1,0:T(8,128)(2,1)}, u32[]{:S(2)}, u32[]{:S(2)}) collective-permute-start(bf16[4,32,128]{2,1,0:T(8,128)(2,1)} %get-tuple-element.29), channel_id=1, source_target_pairs={{1,0},{2,1},{3,2},{4,3},{5,4},{6,5},{7,6},{8,7},{9,8},{10,9},{11,1... | collective-permute-start | bytes 98312 | tf_op jit(solution)/shard_map/ppermute | solution.py:26
  35.0 3.1 %collective-permute-start.3 = (bf16[4,32,128]{2,1,0:T(8,128)(2,1)}, bf16[4,32,128]{2,1,0:T(8,128)(2,1)}, u32[]{:S(2)}, u32[]{:S(2)}) collective-permute-start(bf16[4,32,128]{2,1,0:T(8,128)(2,1)} %get-tuple-element.28), channel_id=1, source_target_pairs={{0,1},{1,2},{2,3},{3,4},{4,5},{5,6},{6,7},{7,8},{8,9},{9,10},{10,1... | collective-permute-start | bytes 98312 | tf_op jit(solution)/shard_map/ppermute | solution.py:26
  38.1 1.4 convolution_bitcast_fusion
  40.3 0.7 fusion.73
  41.0 0.0 copy-start.8
  41.0 0.0 copy-start.13
  41.0 0.9 fusion.15
  42.0 0.6 fusion.27
  42.6 1.1 copy.48
  43.8 8.3 %all-to-all-start = ((f32[32,128,32]{1,2,0:T(8,128)}), f32[32,128,32]{1,2,0:T(8,128)}, u32[]{:S(2)}, u32[]{:S(2)}) async-start(f32[32,128,32]{1,2,0:T(8,128)} %copy.48), calls=%async_computation | async-start | bytes 1048576 | tf_op jit(solution)/shard_map/all_to_all | solution.py:98
  52.1 0.1 lt.59
  52.2 1.0 broadcast_select_fusion
  53.2 0.6 fusion.71
  53.8 3.4 %collective-permute-start = (bf16[32,512]{1,0:T(8,128)(2,1)}, bf16[32,512]{1,0:T(8,128)(2,1)}, u32[]{:S(2)}, u32[]{:S(2)}) collective-permute-start(bf16[32,512]{1,0:T(8,128)(2,1)} %get-tuple-element.30), channel_id=1, source_target_pairs={{0,1},{1,2},{2,3},{3,4},{4,5},{5,6},{6,7},{7,8},{8,9},{9,10},{10,1... | collective-permute-start | bytes 98312 | tf_op jit(solution)/shard_map/ppermute | solution.py:17
  57.2 1.9 %collective-permute-start.1 = (bf16[32,512]{1,0:T(8,128)(2,1)}, bf16[32,512]{1,0:T(8,128)(2,1)}, u32[]{:S(2)}, u32[]{:S(2)}) collective-permute-start(bf16[32,512]{1,0:T(8,128)(2,1)} %get-tuple-element.31), channel_id=1, source_target_pairs={{1,0},{2,1},{3,2},{4,3},{5,4},{6,5},{7,6},{8,7},{9,8},{10,9},{11,1... | collective-permute-start | bytes 98312 | tf_op jit(solution)/shard_map/ppermute | solution.py:18
  59.1 2.3 %convolution_bitcast_fusion.1 = f32[32,64,32]{1,2,0:T(8,128)} fusion(bf16[32,64,128]{2,1,0:T(8,128)(2,1)} %param.21, pred[32,128]{1,0:T(8,128)(4,1)S(1)} %iota_compare_fusion, bf16[32,4096]{1,0:T(8,128)(2,1)} %param.16), kind=kOutput, calls=%fused_computation.12 | convolution fusion | flops 16908288 | bytes 1052672 | tf_op jit(solution)/shard_map/ckb,rcb->ckr/dot_general | solution.py:76
  61.4 1.0 convolution_bitcast_fusion.5
  62.5 1.8 %fusion.72 = f32[32,128,1]{1,0,2:T(8,128)S(1)} fusion(f32[32,64,32]{1,2,0:T(8,128)} %convolution_bitcast_fusion.1, f32[32,64,128]{2,1,0:T(8,128)S(1)} %copy-done.1), kind=kOutput, calls=%fused_computation.97 | convolution fusion | flops 100663296 | bytes 1327104 | tf_op jit(solution)/shard_map/ckq,ckr->qr/dot_general | solution.py:82
  64.3 0.0 copy-start.9
  64.3 0.6 copy-done.9
  64.9 1.0 convolution_bitcast_fusion.6
  65.9 0.6 maximum_bitcast_fusion.1
  66.5 22.8 %psum.7 = f32[1,2,128,32]{2,3,1,0:T(8,128)} all-reduce(f32[1,2,128,32]{2,3,1,0:T(8,128)} %maximum_bitcast_fusion.1), channel_id=1, replica_groups=mesh['slab'=4,'leaf'=8] {'leaf'}, use_global_device_ids=true, to_apply=%region_0.1 | all-reduce | flops 8192 | bytes 65536 | tf_op jit(solution)/shard_map/psum | solution.py:107
  89.3 10.2 %all_gather.7 = f32[4,2,128,32]{2,3,1,0:T(8,128)} all-gather(f32[1,2,128,32]{2,3,1,0:T(8,128)} %psum.7), channel_id=1, replica_groups=mesh['slab'=4,'leaf'=8] {'slab'}, dimensions={0}, use_global_device_ids=true | all-gather | bytes 163840 | tf_op jit(solution)/shard_map/all_gather | solution.py:108
  99.5 1.8 %convolution_bitcast_fusion.3 = f32[128,32]{0,1:T(8,128)} fusion(f32[4,4,128,128]{3,2,1,0:T(8,128)} %param.27, s32[]{:T(128)S(6)} %select_n.42, f32[4,2,128,32]{2,3,1,0:T(8,128)} %all_gather.7, f32[4]{0:T(128)S(1)} %compare_convert_fusion), kind=kOutput, calls=%fused_computation.28 | convolution fusion | flops 25182208 | bytes 344084 | tf_op jit(solution)/shard_map/s,sab,sar->br/dot_general | solution.py:119
  101.3 1.4 convolution_bitcast_fusion.4
  102.7 46.4 %all-gather = f32[4096,32]{0,1:T(8,128)S(1)} all-gather(f32[128,32]{0,1:T(8,128)} %bitcast.174), channel_id=2, replica_groups=mesh['slab'=4,'leaf'=8] {'slab','leaf'}, dimensions={0}, use_global_device_ids=true | all-gather | bytes 540672 | tf_op jit(solution)/shard_map/all_gather | solution.py:87
  149.1 0.1 copy.58
  149.2 1.0 fusion.58
  150.3 1.6 fusion.20
  151.9 0.2 fusion.25
  152.1 3.6 %fusion.18 = bf16[32,64,32]{1,2,0:T(8,128)(2,1)} fusion(f32[32,128,1]{1,0,2:T(8,128)S(1)} %fusion.25, f32[32,64,128]{2,1,0:T(8,128)S(1)} %copy-done.1), kind=kOutput, calls=%fused_computation.22 | convolution fusion | flops 100728832 | bytes 1196032 | tf_op jit(solution)/shard_map/ckq,qr->ckr/dot_general | solution.py:128
  155.7 0.1 copy.39
  155.8 0.1 reshape.124
  155.9 0.8 slice.86
  156.8 0.1 copy.38
  156.9 0.8 copy_bitcast_fusion.2
  157.7 2.2 %gather_fusion = bf16[256,32,128]{2,1,0:T(8,128)(2,1)} fusion(bf16[32,40,128]{2,0,1:T(8,128)(2,1)S(1)} %copy_bitcast_fusion.2, s32[1024]{0:T(1024)S(1)} %pad_clamp_fusion), kind=kCustom, calls=%fused_computation | custom fusion | bytes 4195328 | tf_op jit(solution)/shard_map/jit(_take)/gather | solution.py:59
  159.9 1.4 fusion.44
  161.3 6.9 %fusion.8 = f32[32,32,128]{2,1,0:T(8,128)S(1)} fusion(bf16[32,8,128,128]{3,2,1,0:T(8,128)(2,1)} %param.18, bf16[32,8,32,128]{3,2,1,0:T(8,128)(2,1)} %bitcast.169, pred[32,8]{1,0:T(8,128)(4,1)S(1)} %copy.38), kind=kOutput, calls=%fused_computation.10 | convolution fusion | flops 269484032 | bytes 11010304 | tf_op jit(solution)/shard_map/csab,rcsb->rca/dot_general | solution.py:60
  168.3 0.0 copy-done.3
  168.3 0.0 copy-start.6
  168.3 0.0 copy-start.2
  168.3 0.3 fusion.14
  168.6 0.8 copy.76
  169.4 1.5 fusion.43
  170.9 1.1 reduce_sum.9
  172.0 0.2 fusion.24
  172.2 0.0 copy-done.2
  172.2 2.9 %fusion.19 = bf16[32,64,32]{1,2,0:T(8,128)(2,1)S(1)} fusion(f32[128,32,1]{0,1,2:T(8,128)S(1)} %fusion.24, f32[32,64,128]{2,1,0:T(8,128)S(1)} %copy-done.2), kind=kOutput, calls=%fused_computation.23 | convolution fusion | flops 100728832 | bytes 1196032 | tf_op jit(solution)/shard_map/ckq,qr->ckr/dot_general | solution.py:131
  175.2 1.3 fusion.12
  176.5 0.8 copy.75
  (27 shorter events, 0.1 us)
Async XLA Ops:
  0.6 40.4 %copy-start = (f32[1,24,128,128]{3,2,1,0:T(8,128)S(1)}, f32[1,24,128,128]{3,2,1,0:T(8,128)}, u32[]{:S(2)}) copy-start(f32[1,24,128,128]{3,2,1,0:T(8,128)} %param.25) | copy-start | bytes 4718596
  9.1 29.0 %copy-start.4 = (bf16[32,4096]{1,0:T(8,128)(2,1)S(1)}, bf16[32,4096]{1,0:T(8,128)(2,1)}, u32[]{:S(2)}) copy-start(bf16[32,4096]{1,0:T(8,128)(2,1)} %param.17) | copy-start | bytes 786436
  31.7 8.5 %copy-start.1 = (f32[32,64,128]{2,1,0:T(8,128)S(1)}, f32[32,64,128]{2,1,0:T(8,128)}, u32[]{:S(2)}) copy-start(f32[32,64,128]{2,1,0:T(8,128)} %param.22) | copy-start | bytes 3145732
  32.4 127.5 %collective-permute-start.2 = (bf16[4,32,128]{2,1,0:T(8,128)(2,1)}, bf16[4,32,128]{2,1,0:T(8,128)(2,1)}, u32[]{:S(2)}, u32[]{:S(2)}) collective-permute-start(bf16[4,32,128]{2,1,0:T(8,128)(2,1)} %get-tuple-element.29), channel_id=1, source_target_pairs={{1,0},{2,1},{3,2},{4,3},{5,4},{6,5},{7,6},{8,7},{9,8},{10,9},{11,1... | collective-permute-start | bytes 98312 | tf_op jit(solution)/shard_map/ppermute | solution.py:26
  35.0 134.4 %collective-permute-start.3 = (bf16[4,32,128]{2,1,0:T(8,128)(2,1)}, bf16[4,32,128]{2,1,0:T(8,128)(2,1)}, u32[]{:S(2)}, u32[]{:S(2)}) collective-permute-start(bf16[4,32,128]{2,1,0:T(8,128)(2,1)} %get-tuple-element.28), channel_id=1, source_target_pairs={{0,1},{1,2},{2,3},{3,4},{4,5},{5,6},{6,7},{7,8},{8,9},{9,10},{10,1... | collective-permute-start | bytes 98312 | tf_op jit(solution)/shard_map/ppermute | solution.py:26
  39.5 2.4 %copy-start.11 = (s32[1,24]{1,0:T(1,128)S(1)}, s32[1,24]{1,0:T(1,128)}, u32[]{:S(2)}) copy-start(s32[1,24]{1,0:T(1,128)} %param.23) | copy-start | bytes 292
  40.2 2.4 %copy-start.12 = (pred[24]{0:T(512)(128)(4,1)}, pred[24]{0:T(512)(128)(4,1)S(1)}, u32[]{:S(2)}) copy-start(pred[24]{0:T(512)(128)(4,1)S(1)} %iota_compare_fusion.2) | copy-start | bytes 76
  41.0 2.7 %copy-start.8 = (f32[32,128,1]{1,0,2:T(8,128)}, f32[32,128,1]{1,0,2:T(8,128)S(1)}, u32[]{:S(2)}) copy-start(f32[32,128,1]{1,0,2:T(8,128)S(1)} %fusion.73) | copy-start | bytes 49156
  41.0 11.1 %copy-start.13 = (s32[32]{0:T(128)S(1)}, s32[32]{0:T(128)}, u32[]{:S(2)}) copy-start(s32[32]{0:T(128)} %param.20) | copy-start | bytes 388
  43.8 127.1 %all-to-all-start = ((f32[32,128,32]{1,2,0:T(8,128)}), f32[32,128,32]{1,2,0:T(8,128)}, u32[]{:S(2)}, u32[]{:S(2)}) async-start(f32[32,128,32]{1,2,0:T(8,128)} %copy.48), calls=%async_computation | async-start | bytes 1048576 | tf_op jit(solution)/shard_map/all_to_all | solution.py:98
  53.8 103.0 %collective-permute-start = (bf16[32,512]{1,0:T(8,128)(2,1)}, bf16[32,512]{1,0:T(8,128)(2,1)}, u32[]{:S(2)}, u32[]{:S(2)}) collective-permute-start(bf16[32,512]{1,0:T(8,128)(2,1)} %get-tuple-element.30), channel_id=1, source_target_pairs={{0,1},{1,2},{2,3},{3,4},{4,5},{5,6},{6,7},{7,8},{8,9},{9,10},{10,1... | collective-permute-start | bytes 98312 | tf_op jit(solution)/shard_map/ppermute | solution.py:17
  57.2 99.7 %collective-permute-start.1 = (bf16[32,512]{1,0:T(8,128)(2,1)}, bf16[32,512]{1,0:T(8,128)(2,1)}, u32[]{:S(2)}, u32[]{:S(2)}) collective-permute-start(bf16[32,512]{1,0:T(8,128)(2,1)} %get-tuple-element.31), channel_id=1, source_target_pairs={{1,0},{2,1},{3,2},{4,3},{5,4},{6,5},{7,6},{8,7},{9,8},{10,9},{11,1... | collective-permute-start | bytes 98312 | tf_op jit(solution)/shard_map/ppermute | solution.py:18
  64.3 0.6 copy-start.9
  149.1 2.8 %copy-start.5 = (f32[1,128,128]{2,1,0:T(8,128)S(1)}, f32[1,128,128]{2,1,0:T(8,128)}, u32[]{:S(2)}) copy-start(f32[1,128,128]{2,1,0:T(8,128)} %param.26) | copy-start | bytes 196612
  161.3 7.0 %copy-start.3 = (bf16[32,64,128]{2,1,0:T(8,128)(2,1)S(1)}, bf16[32,64,128]{2,1,0:T(8,128)(2,1)}, u32[]{:S(2)}) copy-start(bf16[32,64,128]{2,1,0:T(8,128)(2,1)} %param.21) | copy-start | bytes 1572868
  161.3 7.0 %copy-start.7 = (bf16[32,64,32]{1,2,0:T(8,128)(2,1)S(1)}, bf16[32,64,32]{1,2,0:T(8,128)(2,1)}, u32[]{:S(2)}) copy-start(bf16[32,64,32]{1,2,0:T(8,128)(2,1)} %fusion.18) | copy-start | bytes 393220
  168.3 3.7 %copy-start.6 = (f32[1,128,128]{2,1,0:T(8,128)S(1)}, f32[1,128,128]{2,1,0:T(8,128)}, u32[]{:S(2)}) copy-start(f32[1,128,128]{2,1,0:T(8,128)} %param.26) | copy-start | bytes 196612
  168.3 3.7 %copy-start.10 = (f32[128,32]{0,1:T(8,128)S(1)}, f32[128,32]{0,1:T(8,128)}, u32[]{:S(2)}) copy-start(f32[128,32]{0,1:T(8,128)} %convolution_bitcast_fusion.3) | copy-start | bytes 49156
  168.3 3.9 %copy-start.2 = (f32[32,64,128]{2,1,0:T(8,128)S(1)}, f32[32,64,128]{2,1,0:T(8,128)}, u32[]{:S(2)}) copy-start(f32[32,64,128]{2,1,0:T(8,128)} %param.22) | copy-start | bytes 3145732
where the time goes:
time: 180 us; the launch traced here: 177 us
  blocking collectives  79.4 us (44%)
  matrix products  37.8 us (21%)
  other arithmetic  30.6 us (17%)
  starting transfers between devices  19.3 us (11%)
  local copies, waits for them, and re-layouts  8.43 us (5%)
    all_gather x1, blocking collectives, shards(): lax.all_gather(parent_right[None], ('slab', 'leaf'), axis=0, tiled=True)  46.4 us
    psum x1, blocking collectives, shards(): within = lax.psum(slab_share, 'leaf')  22.8 us
    scatter-add x1, other arithmetic, shards(): jax.ops.segment_sum(contrib.reshape(-1, rhs_count, B), offsets.reshape(-1...  22.6 us
    all_gather x1, blocking collectives, shards(): slab_sum_totals = lax.all_gather(within[None], 'slab', axis=0, tiled=True)  10.2 us
    all_to_all x1, starting transfers between devices, shards(): lax.all_to_all(spread, ('slab', 'leaf'), split_axis=0, concat_axis=0, til...  8.33 us
    dot_general x1, matrix products, shards(): jnp.einsum('csab,rcsb->rca', near_blocks, picked, preferred_element_type=...  6.94 us
    dot_general x1, matrix products, shards(): jnp.einsum('csab,rca->csrb', near_blocks, masked_left, preferred_element_...  6.65 us
    ppermute x2, starting transfers between devices, passed_along(): return lax.ppermute(block, axis, route)  5.67 us
  transfers between devices with their start and end apart: 5, of which 0 were waited for; matrix products, arithmetic and copies ran while one was open for 21% of the time, Pallas kernels for 0%

commit v1 on v0

v1 whole, which is shorter than its diff:
```python
import functools

import jax
import jax.numpy as jnp
from jax import lax
from jax.experimental import pallas as pl
from jax.experimental.pallas import tpu as pltpu
from jax.sharding import PartitionSpec as P

B = 128
HW = 4
BF = jnp.bfloat16
F32 = jnp.float32
MESH = pl.DeviceIdType.MESH


def nt(a, b):
    return lax.dot_general(a, b, (((1,), (1,)), ((), ())), preferred_element_type=F32)


def nn(a, b):
    return lax.dot_general(a, b, (((1,), (0,)), ((), ())), preferred_element_type=F32)


def split(x):
    high = x.astype(BF)
    return high, (x - high.astype(F32)).astype(BF)


def three(a, b, product):
    rows = a.shape[0]
    ah, al = split(a)
    bh, bl = split(b)
    both = product(jnp.concatenate([ah, al], axis=0), bh)
    return both[:rows] + both[rows:] + product(ah, bl)


def kernel(
    slabs,
    leaves,
    points_s,
    columns_s,
    inverse_s,
    targets_s,
    count_s,
    far_inverse_s,
    right_h,
    left_h,
    basis_h,
    transfer_h,
    lift_h,
    coupling_h,
    apex_h,
    near_h,
    product_ref,
    adjoint_ref,
    right_v,
    left_v,
    basis_v,
    transfer_v,
    lift_v,
    coupling_v,
    apex_row_v,
    apex_col_v,
    near_v,
    ext_v,
    masked_left_v,
    collected_v,
    near_out_v,
    edge_out_v,
    edge_in_v,
    share_v,
    share_in_v,
    slab_v,
    parents_v,
    outward_v,
    arrived_v,
    down_v,
    in_sem,
    halo_send,
    halo_recv,
    edge_send,
    edge_recv,
    share_send,
    share_recv,
    slab_send,
    slab_recv,
    parent_send,
    parent_recv,
    out_send,
    out_recv,
):
    rhs = right_h.shape[0]
    clusters, slots = near_v.shape[:2]
    rank = basis_v.shape[1]
    far_slots = coupling_v.shape[0]
    devices = slabs * leaves
    width = 2 * HW + 1
    my_slab = lax.axis_index("slab")
    my_leaf = lax.axis_index("leaf")
    me = my_slab * leaves + my_leaf
    first = 1 - (me + devices - 1) // devices
    last = (me + 1) // devices

    def place(d):
        return (d // leaves, d % leaves)

    ext_v[0:HW] = jnp.zeros((HW, rhs, B), BF)
    ext_v[clusters + HW :] = jnp.zeros((HW, rhs, B), BF)
    edge_in_v[...] = jnp.zeros_like(edge_in_v)

    inputs = [
        pltpu.make_async_copy(src, dst, in_sem.at[i])
        for i, (src, dst) in enumerate(
            [
                (right_h, right_v),
                (left_h, left_v),
                (basis_h, basis_v),
                (transfer_h, transfer_v),
                (lift_h, lift_v),
                (coupling_h, coupling_v),
                (near_h, near_v),
                (apex_h.at[my_slab], apex_row_v),
                (apex_h.at[:, my_slab], apex_col_v),
            ]
        )
    ]
    for copy in inputs:
        copy.start()

    barrier = pltpu.get_barrier_semaphore()

    def greet(k, _):
        pl.semaphore_signal(
            barrier, inc=1, device_id=place((me + k) % devices), device_id_type=MESH
        )
        return 0

    lax.fori_loop(1, devices, greet, 0)

    collected_v[...] = jnp.zeros_like(collected_v)
    for copy in inputs[:4]:
        copy.wait()

    lane = lax.broadcasted_iota(jnp.int32, (rhs, B), 1)

    def window(c):
        return pl.ds(pl.multiple_of(c * B, B), B)

    def mask_of(c):
        return jnp.where(lane < points_s[c], 1.0, 0.0)

    def leaf_step(c, total):
        mask = mask_of(c).astype(BF)
        r = right_v[:, window(c)] * mask
        l = left_v[:, window(c)] * mask
        ext_v[c + HW] = r
        masked_left_v[c] = l
        leaf = nt(jnp.concatenate([r, l], axis=0), basis_v[c])
        return total + three(leaf, transfer_v[c], nn)

    unroll = 4

    def leaf_group(g, total):
        for u in range(unroll):
            total = leaf_step(g * unroll + u, total)
        return total

    parent = lax.fori_loop(
        0, clusters // unroll, leaf_group, jnp.zeros((2 * rhs, transfer_v.shape[2]), F32)
    )

    parents_v[me] = parent[:rhs].astype(BF)
    inputs[4].wait()
    share = three(parent, lift_v[...], nn)
    chunk = share_v.shape[1]
    for j in range(leaves):
        share_v[j] = share[j * chunk : (j + 1) * chunk]

    pl.semaphore_wait(barrier, devices - 1)

    def halo_copy(to_next):
        where = me + 1 if to_next else me - 1
        src = clusters if to_next else HW
        dst = 0 if to_next else clusters + HW
        i = 0 if to_next else 1
        return pltpu.make_async_remote_copy(
            src_ref=ext_v.at[pl.ds(src, HW)],
            dst_ref=ext_v.at[pl.ds(dst, HW)],
            send_sem=halo_send.at[i],
            recv_sem=halo_recv.at[i],
            device_id=place(where),
            device_id_type=MESH,
        )

    def share_copy(k):
        peer = (my_leaf + k) % leaves
        return pltpu.make_async_remote_copy(
            src_ref=share_v.at[peer],
            dst_ref=share_in_v.at[my_leaf],
            send_sem=share_send.at[k],
            recv_sem=share_recv.at[k],
            device_id=(my_slab, peer),
            device_id_type=MESH,
        )

    def share_arrival(k):
        peer = (my_leaf + leaves - k) % leaves
        return pltpu.make_async_remote_copy(
            src_ref=share_v.at[my_leaf],
            dst_ref=share_in_v.at[peer],
            send_sem=share_send.at[k],
            recv_sem=share_recv.at[k],
            device_id=(my_slab, peer),
            device_id_type=MESH,
        )

    def wide_copy(k, src, dst, send, recv, spread):
        peer = (me + k) % devices
        return pltpu.make_async_remote_copy(
            src_ref=src.at[peer if spread else me],
            dst_ref=dst.at[me],
            send_sem=send.at[k],
            recv_sem=recv.at[k],
            device_id=place(peer),
            device_id_type=MESH,
        )

    def wide_arrival(k, src, dst, send, recv):
        peer = (me + devices - k) % devices
        return pltpu.make_async_remote_copy(
            src_ref=src.at[me],
            dst_ref=dst.at[peer],
            send_sem=send.at[k],
            recv_sem=recv.at[k],
            device_id=place(peer),
            device_id_type=MESH,
        )

    def loop(low, high, act):
        def step(k, carry):
            act(k)
            return carry

        lax.fori_loop(low, high, step, 0)

    loop(1, leaves, lambda k: share_copy(k).start())
    share_in_v[my_leaf] = share_v[my_leaf]

    @pl.when(me < devices - 1)
    def _():
        halo_copy(True).start()

    @pl.when(me > 0)
    def _():
        halo_copy(False).start()

    inputs[5].wait()
    lh, ll = split(parent[rhs:])
    left_both = jnp.concatenate([lh, ll], axis=0)

    def outward(q):
        f = far_inverse_s[q]
        live = jnp.where(f >= 0, 1.0, 0.0)
        ch, cl = split(coupling_v[jnp.maximum(f, 0)])
        both = nn(left_both, ch)
        term = both[:rhs] + both[rhs:] + nn(lh, cl)
        outward_v[q] = (term * live).astype(BF)

    def outward_group(g):
        for u in range(unroll):
            outward(g * unroll + u)

    loop(0, devices // unroll, outward_group)
    arrived_v[me] = jnp.zeros((rhs, arrived_v.shape[2]), BF)

    loop(1, leaves, lambda k: share_arrival(k).wait_recv())
    total = share_in_v[0]
    for j in range(1, leaves):
        total = total + share_in_v[j]
    slab_v[me] = total

    loop(1, devices, lambda k: wide_copy(k, slab_v, slab_v, slab_send, slab_recv, False).start())
    loop(
        1,
        devices,
        lambda k: wide_copy(k, parents_v, parents_v, parent_send, parent_recv, False).start(),
    )
    loop(
        1,
        devices,
        lambda k: wide_copy(k, outward_v, arrived_v, out_send, out_recv, True).start(),
    )

    inputs[6].wait()

    def near_back(i, e0):
        left = masked_left_v[i]
        for w in range(width):
            s = inverse_s[i * width + w]
            live = jnp.where(s >= 0, 1.0, 0.0)
            term = nn(left, near_v[i, jnp.maximum(s, 0)])
            collected_v[e0 + w] += term * live

    def near_forward(i):
        total = None
        for s in range(slots):
            term = nt(ext_v[columns_s[i * slots + s]], near_v[i, s])
            total = term if total is None else total + term
        near_out_v[i] = total

    for i in range(HW):
        near_back(i, i + first * (HW - i))
    for i in range(clusters - HW, clusters):
        near_back(i, i - last * (i - (clusters - HW - 1)))

    edge_out_v[0] = collected_v[0:HW].astype(BF)
    edge_out_v[1] = collected_v[clusters + HW :].astype(BF)

    def edge_copy(to_next):
        i = 1 if to_next else 0
        return pltpu.make_async_remote_copy(
            src_ref=edge_out_v.at[i],
            dst_ref=edge_in_v.at[i],
            send_sem=edge_send.at[i],
            recv_sem=edge_recv.at[i],
            device_id=place(me + 1 if to_next else me - 1),
            device_id_type=MESH,
        )

    @pl.when(me < devices - 1)
    def _():
        edge_copy(True).start()

    @pl.when(me > 0)
    def _():
        edge_copy(False).start()

    @pl.when(me > 0)
    def _():
        halo_copy(True).wait_recv()

    @pl.when(me < devices - 1)
    def _():
        halo_copy(False).wait_recv()

    for i in list(range(HW)) + list(range(clusters - HW, clusters)):
        near_forward(i)

    def middle(i):
        near_back(i, i)
        near_forward(i)

    loop(HW, clusters - HW, middle)

    @pl.when(me > 0)
    def _():
        edge_copy(True).wait_recv()

    @pl.when(me < devices - 1)
    def _():
        edge_copy(False).wait_recv()

    collected_v[HW : 2 * HW] += edge_in_v[1].astype(F32)
    collected_v[clusters : clusters + HW] += edge_in_v[0].astype(F32)

    loop(1, devices, lambda k: wide_arrival(k, slab_v, slab_v, slab_send, slab_recv).wait_recv())
    inputs[7].wait()
    inputs[8].wait()
    apex_right = jnp.zeros((rhs, lift_v.shape[1]), F32)
    apex_left = jnp.zeros((rhs, lift_v.shape[1]), F32)
    for t in range(slabs):
        other = jnp.where(my_slab == t, 0.0, 1.0)
        whole = jnp.concatenate([slab_v[t * leaves + j] for j in range(leaves)], axis=0)
        apex_right += other * three(whole[:rhs], apex_row_v[t], nt)
        apex_left += other * three(whole[rhs:], apex_col_v[t], nn)
    spread = three(jnp.concatenate([apex_right, apex_left], axis=0), lift_v[...], nt)

    loop(
        1,
        devices,
        lambda k: wide_arrival(k, parents_v, parents_v, parent_send, parent_recv).wait_recv(),
    )

    def far(f, total):
        live = jnp.where(f < count_s[0], 1.0, 0.0)
        ch, cl = split(coupling_v[f])
        chosen = parents_v[targets_s[f]]
        return total + live * (nt(chosen, ch) + nt(chosen, cl))

    def far_group(g, total):
        for u in range(unroll):
            total = far(g * unroll + u, total)
        return total

    far_right = lax.fori_loop(0, far_slots // unroll, far_group, spread[:rhs])

    loop(
        1, devices, lambda k: wide_arrival(k, outward_v, arrived_v, out_send, out_recv).wait_recv()
    )
    far_left = lax.fori_loop(
        0, devices, lambda d, total: total + arrived_v[d].astype(F32), spread[rhs:]
    )

    hat = jnp.concatenate([far_right, far_left], axis=0)
    hh, hl = split(hat)
    hat_both = jnp.concatenate([hh, hl], axis=0)

    def finish(c):
        th, tl = split(transfer_v[c])
        both = nt(hat_both, th)
        down = (both[: 2 * rhs] + both[2 * rhs :] + nt(hh, tl)).astype(BF)
        out = nn(down, basis_v[c])
        keep = lane < points_s[c]
        product_ref[:, window(c)] = jnp.where(keep, near_out_v[c] + out[:rhs], 0.0)
        adjoint_ref[:, window(c)] = jnp.where(keep, collected_v[c + HW] + out[rhs:], 0.0)

    def finish_group(g):
        for u in range(unroll):
            finish(g * unroll + u)

    loop(0, clusters // unroll, finish_group)

    loop(1, leaves, lambda k: share_copy(k).wait_send())
    loop(1, devices, lambda k: wide_copy(k, slab_v, slab_v, slab_send, slab_recv, False).wait_send())
    loop(
        1,
        devices,
        lambda k: wide_copy(k, parents_v, parents_v, parent_send, parent_recv, False).wait_send(),
    )
    loop(
        1,
        devices,
        lambda k: wide_copy(k, outward_v, arrived_v, out_send, out_recv, True).wait_send(),
    )

    @pl.when(me < devices - 1)
    def _():
        halo_copy(True).wait_send()
        edge_copy(True).wait_send()

    @pl.when(me > 0)
    def _():
        halo_copy(False).wait_send()
        edge_copy(False).wait_send()


def shards(
    right_sides,
    left_sides,
    near_blocks,
    near_columns,
    cluster_points,
    leaf_basis,
    transfer,
    far_parents,
    far_count,
    coupling,
    slab_transfer,
    apex_coupling,
):
    slabs, leaves = lax.axis_size("slab"), lax.axis_size("leaf")
    devices = slabs * leaves
    rhs, columns = right_sides.shape
    clusters, slots = near_columns.shape
    rank, k2 = transfer.shape[1:]
    k3 = slab_transfer.shape[2]
    far_slots = coupling.shape[1]
    width = 2 * HW + 1
    me = lax.axis_index(("slab", "leaf"))
    rows = me * clusters + jnp.arange(clusters, dtype=jnp.int32)
    start = jnp.clip(rows - HW, 0, devices * clusters - width)
    wanted = start[:, None] + jnp.arange(width, dtype=jnp.int32)[None, :]
    number = jnp.arange(1, slots + 1, dtype=jnp.int32)
    inverse = (
        jnp.sum(jnp.where(near_columns[:, None, :] == wanted[:, :, None], number, 0), axis=2) - 1
    )
    f_index = jnp.arange(far_slots, dtype=jnp.int32)
    hit = (far_parents[0][None, :] == jnp.arange(devices, dtype=jnp.int32)[:, None]) & (
        f_index < far_count[0]
    )[None, :]
    far_inverse = jnp.sum(jnp.where(hit, f_index + 1, 0), axis=1) - 1

    chunk = 2 * rhs // leaves
    smem = pl.BlockSpec(memory_space=pltpu.SMEM)
    hbm = pl.BlockSpec(memory_space=pl.ANY)
    vmem = pl.BlockSpec(memory_space=pltpu.VMEM)
    dma = pltpu.SemaphoreType.DMA
    out = jax.ShapeDtypeStruct((rhs, columns), F32)
    return pl.pallas_call(
        functools.partial(kernel, slabs, leaves),
        out_shape=(out, out),
        in_specs=[smem] * 6 + [hbm] * 8,
        out_specs=(vmem, vmem),
        scratch_shapes=[
            pltpu.VMEM((rhs, columns), BF),
            pltpu.VMEM((rhs, columns), BF),
            pltpu.VMEM(leaf_basis.shape, BF),
            pltpu.VMEM(transfer.shape, F32),
            pltpu.VMEM((k2, k3), F32),
            pltpu.VMEM(coupling.shape[1:], F32),
            pltpu.VMEM((slabs, k3, k3), F32),
            pltpu.VMEM((slabs, k3, k3), F32),
            pltpu.VMEM(near_blocks.shape, BF),
            pltpu.VMEM((clusters + 2 * HW, rhs, B), BF),
            pltpu.VMEM((clusters, rhs, B), BF),
            pltpu.VMEM((clusters + 2 * HW, rhs, B), F32),
            pltpu.VMEM((clusters, rhs, B), F32),
            pltpu.VMEM((2, HW, rhs, B), BF),
            pltpu.VMEM((2, HW, rhs, B), BF),
            pltpu.VMEM((leaves, chunk, k3), F32),
            pltpu.VMEM((leaves, chunk, k3), F32),
            pltpu.VMEM((devices, chunk, k3), F32),
            pltpu.VMEM((devices, rhs, k2), BF),
            pltpu.VMEM((devices, rhs, k2), BF),
            pltpu.VMEM((devices, rhs, k2), BF),
            pltpu.VMEM((2 * rhs, rank), BF),
            dma((9,)),
            dma((2,)),
            dma((2,)),
            dma((2,)),
            dma((2,)),
            dma((leaves,)),
            dma((leaves,)),
            dma((devices,)),
            dma((devices,)),
            dma((devices,)),
            dma((devices,)),
            dma((devices,)),
            dma((devices,)),
        ],
        compiler_params=pltpu.CompilerParams(
            collective_id=0, has_side_effects=True, vmem_limit_bytes=48 * 1024 * 1024
        ),
        name="h2_step",
    )(
        cluster_points,
        (near_columns - (me * clusters - HW)).reshape(-1),
        inverse.reshape(-1),
        far_parents[0],
        far_count,
        far_inverse,
        right_sides,
        left_sides,
        leaf_basis,
        transfer,
        slab_transfer[0],
        coupling[0],
        apex_coupling,
        near_blocks,
    )


def solution(mesh):
    return jax.shard_map(
        shards,
        mesh=mesh,
        in_specs=(
            P(None, ("slab", "leaf")),
            P(None, ("slab", "leaf")),
            P(("slab", "leaf"), None, None, None),
            P(("slab", "leaf"), None),
            P(("slab", "leaf")),
            P(("slab", "leaf"), None, None),
            P(("slab", "leaf"), None, None),
            P(("slab", "leaf"), None),
            P(("slab", "leaf")),
            P(("slab", "leaf"), None, None, None),
            P(("slab", "leaf"), None, None),
            P(),
        ),
        out_specs=(P(None, ("slab", "leaf")), P(None, ("slab", "leaf"))),
        check_vma=False,
    )
```

time: 180 us -> 52.8 us (0.29); the launches traced: 177 us -> 52.3 us
  blocking collectives: 79.4 us -> 0 us
  matrix products: 37.8 us -> 0 us
  Pallas kernels: 0 us -> 37.8 us
  other arithmetic: 30.6 us -> 2.25 us
  starting transfers between devices: 19.3 us -> 0 us
  local copies, waits for them, and re-layouts: 8.43 us -> 10.9 us
    all_gather x2 -> x0, blocking collectives: 56.6 us -> none  [the longest x1 46.4 us: shards(): lax.all_gather(parent_right[None], ('slab', 'leaf'), axis=0, tiled=True)]
    pallas_call x0 -> x1, Pallas kernels: none -> 37.8 us  [shards(): pl.pallas_call(functools.partial(kernel, slabs, leaves), out_shape=(out,...]
    dot_general x20 -> x0, matrix products: 37.8 us -> none  [the longest x1 6.94 us: shards(): jnp.einsum('csab,rcsb->rca', near_blocks, picked, preferred_element_type=...]
    scatter-add x3 -> x0, other arithmetic: 25.5 us -> none  [the longest x1 22.6 us: shards(): jax.ops.segment_sum(contrib.reshape(-1, rhs_count, B), offsets.reshape(-1...]
    psum x1 -> x0, blocking collectives: 22.8 us -> none  [shards(): within = lax.psum(slab_share, 'leaf')]
    ppermute x4 -> x0, starting transfers between devices: 11 us -> none  [the longest x2 5.67 us: passed_along(): return lax.ppermute(block, axis, route)]
    unnamed x29 -> x20, local copies, waits for them, and re-layouts: 0.79 us -> 10.5 us
    all_to_all x1 -> x0, starting transfers between devices: 8.33 us -> none  [shards(): lax.all_to_all(spread, ('slab', 'leaf'), split_axis=0, concat_axis=0, til...]
  transfers between devices with their start and end apart: 5 -> 0, of which waited for: 0 -> 0; matrix products, arithmetic and copies ran while one was open for 21% -> 0% of each run, Pallas kernels for 0% -> 0%
where the time goes in v1:
time: 52.8 us; the launch traced here: 52.3 us
  Pallas kernels  37.8 us (72%)
  local copies, waits for them, and re-layouts  10.9 us (21%)
  other arithmetic  2.25 us (4%)
  between operations  1.35 us (3%)
    pallas_call x1, Pallas kernels, shards(): pl.pallas_call(functools.partial(kernel, slabs, leaves), out_shape=(out,...  37.8 us
    unnamed x20, local copies, waits for them, and re-layouts  10.5 us

profile of v1, /device:TPU:9, one launch (start us, length us, event | category | flops | bytes accessed | tf_op | source)
XLA Modules:
  0.0 52.3 jit_solution(6372079422666790179)
XLA Ops:
  1.3 0.7 %select_reduce_fusion.1 = s32[32]{0:T(128)S(1)} fusion(s32[24]{0:T(128)S(1)} %iota_add_fusion.1, s32[24]{0:T(128)} %bitcast.7, pred[24]{0:T(512)(128)(4,1)S(1)} %iota_compare_fusion.1), kind=kLoop, calls=%fused_computation.1 | loop fusion | flops 3040 | bytes 344 | tf_op jit(solution)/shard_map/reduce_sum | solution.py:482
  2.1 0.7 %broadcast_subtract_fusion = s32[32,8]{0,1:T(8,128)S(1)} fusion(s32[32,8]{0,1:T(8,128)} %param.15, s32[]{:T(128)S(6)} %sub.23), kind=kLoop, calls=%fused_computation.6 | loop fusion | flops 256 | bytes 2052 | tf_op jit(solution)/shard_map/sub | solution.py:538
  2.8 0.8 %select_reduce_fusion = s32[32,9]{0,1:T(8,128)S(1)} fusion(s32[8]{0:T(128)S(1)} %iota_add_fusion.2, s32[32,9]{0,1:T(8,128)S(1)} %iota_add_fusion, s32[32,8]{0,1:T(8,128)} %param.15), kind=kLoop, calls=%fused_computation | loop fusion | flops 6624 | bytes 3360 | tf_op jit(solution)/shard_map/reduce_sum | solution.py:476
  3.6 0.1 copy.18
  3.7 0.1 sub.28.inverse_s
  3.8 0.1 copy.17
  3.8 0.1 reshape.42.columns_s
  3.9 0.0 copy-start
  3.9 1.4 %copy-done = f32[1,24,128,128]{3,2,1,0:T(8,128)S(1)} copy-done((f32[1,24,128,128]{3,2,1,0:T(8,128)S(1)}, f32[1,24,128,128]{3,2,1,0:T(8,128)}, u32[]{:S(2)}) %copy-start) | copy-done | bytes 1572888
  5.3 0.0 copy-start.1
  5.3 1.2 %copy-done.1 = f32[32,64,128]{2,1,0:T(8,128)S(1)} copy-done((f32[32,64,128]{2,1,0:T(8,128)S(1)}, f32[32,64,128]{2,1,0:T(8,128)}, u32[]{:S(2)}) %copy-start.1) | copy-done | bytes 1048600
  6.6 0.0 copy-start.2
  6.6 1.2 %copy-done.2 = f32[4,4,128,128]{3,2,1,0:T(8,128)S(1)} copy-done((f32[4,4,128,128]{3,2,1,0:T(8,128)S(1)}, f32[4,4,128,128]{3,2,1,0:T(8,128)}, u32[]{:S(2)}) %copy-start.2) | copy-done | bytes 1048600
  7.8 0.0 copy-start.3
  7.8 1.0 %copy-done.3 = bf16[32,64,128]{2,1,0:T(8,128)(2,1)S(1)} copy-done((bf16[32,64,128]{2,1,0:T(8,128)(2,1)S(1)}, bf16[32,64,128]{2,1,0:T(8,128)(2,1)}, u32[]{:S(2)}) %copy-start.3) | copy-done | bytes 524312
  8.8 0.0 copy-start.4
  8.8 0.9 %copy-done.4 = bf16[32,4096]{1,0:T(8,128)(2,1)S(1)} copy-done((bf16[32,4096]{1,0:T(8,128)(2,1)S(1)}, bf16[32,4096]{1,0:T(8,128)(2,1)}, u32[]{:S(2)}) %copy-start.4) | copy-done | bytes 262168
  9.8 0.0 copy-start.5
  9.8 0.9 %copy-done.5 = bf16[32,4096]{1,0:T(8,128)(2,1)S(1)} copy-done((bf16[32,4096]{1,0:T(8,128)(2,1)S(1)}, bf16[32,4096]{1,0:T(8,128)(2,1)}, u32[]{:S(2)}) %copy-start.5) | copy-done | bytes 262168
  10.7 0.0 copy-start.6
  10.7 0.8 %copy-done.6 = f32[1,128,128]{2,1,0:T(8,128)S(1)} copy-done((f32[1,128,128]{2,1,0:T(8,128)S(1)}, f32[1,128,128]{2,1,0:T(8,128)}, u32[]{:S(2)}) %copy-start.6) | copy-done | bytes 65560
  11.6 0.0 copy-start.7
  11.6 0.7 %copy-done.7 = s32[1,24]{1,0:T(1,128)S(1)} copy-done((s32[1,24]{1,0:T(1,128)S(1)}, s32[1,24]{1,0:T(1,128)}, u32[]{:S(2)}) %copy-start.7) | copy-done | bytes 120
  12.2 0.0 copy-start.8
  12.2 0.7 %copy-done.8 = s32[32]{0:T(128)S(1)} copy-done((s32[32]{0:T(128)S(1)}, s32[32]{0:T(128)}, u32[]{:S(2)}) %copy-start.8) | copy-done | bytes 152
  12.9 37.8 %h2_step.1 = (f32[32,4096]{1,0:T(8,128)S(1)}, f32[32,4096]{1,0:T(8,128)S(1)}) custom-call(s32[32]{0:T(128)S(1)} %copy-done.8, s32[256]{0:T(256)S(1)} %reshape.42.columns_s, s32[288]{0:T(512)S(1)} %sub.28.inverse_s, s32[24]{0:T(128)S(1)} %bitcast.8, s32[1]{0:T(128)} %copy.21.count_s, s32[32]{0:T(128)S(1)} %broadcast_add_fusion.1.far_inverse_s, ...), custom_call_target="tpu_custom_call" | custom-call | tf_op jit(solution)/shard_map/h2_step/pallas_call | solution.py:490
  50.7 0.8 %copy.22 = f32[32,4096]{1,0:T(8,128)} copy(f32[32,4096]{1,0:T(8,128)S(1)} %get-tuple-element.4) | data formatting | bytes 1048576
  51.5 0.8 %copy.23 = f32[32,4096]{1,0:T(8,128)} copy(f32[32,4096]{1,0:T(8,128)S(1)} %get-tuple-element.5) | data formatting | bytes 1048576
  (7 shorter events, 0.0 us)
Async XLA Ops:
  3.9 1.4 %copy-start = (f32[1,24,128,128]{3,2,1,0:T(8,128)S(1)}, f32[1,24,128,128]{3,2,1,0:T(8,128)}, u32[]{:S(2)}) copy-start(f32[1,24,128,128]{3,2,1,0:T(8,128)} %param.21) | copy-start | bytes 4718596
  5.3 1.2 %copy-start.1 = (f32[32,64,128]{2,1,0:T(8,128)S(1)}, f32[32,64,128]{2,1,0:T(8,128)}, u32[]{:S(2)}) copy-start(f32[32,64,128]{2,1,0:T(8,128)} %transfer_h.1) | copy-start | bytes 3145732
  6.6 1.2 %copy-start.2 = (f32[4,4,128,128]{3,2,1,0:T(8,128)S(1)}, f32[4,4,128,128]{3,2,1,0:T(8,128)}, u32[]{:S(2)}) copy-start(f32[4,4,128,128]{3,2,1,0:T(8,128)} %apex_h.1) | copy-start | bytes 3145732
  7.8 1.0 %copy-start.3 = (bf16[32,64,128]{2,1,0:T(8,128)(2,1)S(1)}, bf16[32,64,128]{2,1,0:T(8,128)(2,1)}, u32[]{:S(2)}) copy-start(bf16[32,64,128]{2,1,0:T(8,128)(2,1)} %basis_h.1) | copy-start | bytes 1572868
  8.8 0.9 %copy-start.4 = (bf16[32,4096]{1,0:T(8,128)(2,1)S(1)}, bf16[32,4096]{1,0:T(8,128)(2,1)}, u32[]{:S(2)}) copy-start(bf16[32,4096]{1,0:T(8,128)(2,1)} %right_h.1) | copy-start | bytes 786436
  9.8 0.9 %copy-start.5 = (bf16[32,4096]{1,0:T(8,128)(2,1)S(1)}, bf16[32,4096]{1,0:T(8,128)(2,1)}, u32[]{:S(2)}) copy-start(bf16[32,4096]{1,0:T(8,128)(2,1)} %left_h.1) | copy-start | bytes 786436
  10.7 0.8 %copy-start.6 = (f32[1,128,128]{2,1,0:T(8,128)S(1)}, f32[1,128,128]{2,1,0:T(8,128)}, u32[]{:S(2)}) copy-start(f32[1,128,128]{2,1,0:T(8,128)} %param.22) | copy-start | bytes 196612
  11.6 0.7 %copy-start.7 = (s32[1,24]{1,0:T(1,128)S(1)}, s32[1,24]{1,0:T(1,128)}, u32[]{:S(2)}) copy-start(s32[1,24]{1,0:T(1,128)} %param.19) | copy-start | bytes 292
  12.2 0.7 %copy-start.8 = (s32[32]{0:T(128)S(1)}, s32[32]{0:T(128)}, u32[]{:S(2)}) copy-start(s32[32]{0:T(128)} %points_s.1) | copy-start | bytes 388

commit v2 on v1

--- a/solution.py
+++ b/solution.py
@@ -39,11 +39,9 @@
     slabs,
     leaves,
     points_s,
-    columns_s,
-    inverse_s,
     targets_s,
     count_s,
-    far_inverse_s,
+    columns_h,
     right_h,
     left_h,
     basis_h,
@@ -63,6 +61,11 @@
     apex_row_v,
     apex_col_v,
     near_v,
+    columns_v,
+    table_v,
+    far_table_v,
+    table_s,
+    far_table_s,
     ext_v,
     masked_left_v,
     collected_v,
@@ -77,6 +80,7 @@
     arrived_v,
     down_v,
     in_sem,
+    table_sem,
     halo_send,
     halo_recv,
     edge_send,
@@ -91,7 +95,7 @@
     out_recv,
 ):
     rhs = right_h.shape[0]
-    clusters, slots = near_v.shape[:2]
+    slots, clusters = columns_v.shape
     rank = basis_v.shape[1]
     far_slots = coupling_v.shape[0]
     devices = slabs * leaves
@@ -119,13 +123,15 @@
                 (transfer_h, transfer_v),
                 (lift_h, lift_v),
                 (coupling_h, coupling_v),
-                (near_h, near_v),
+                (near_h, near_v.at[pl.ds(0, clusters * slots)]),
                 (apex_h.at[my_slab], apex_row_v),
                 (apex_h.at[:, my_slab], apex_col_v),
+                (columns_h, columns_v),
             ]
         )
     ]
-    for copy in inputs:
+    inputs[9].start()
+    for copy in inputs[:9]:
         copy.start()
 
     barrier = pltpu.get_barrier_semaphore()
@@ -139,6 +145,36 @@
     lax.fori_loop(1, devices, greet, 0)
 
     collected_v[...] = jnp.zeros_like(collected_v)
+    near_v[clusters * slots] = jnp.zeros((B, B), BF)
+
+    inputs[9].wait()
+    row = lax.broadcasted_iota(jnp.int32, (1, clusters), 1)
+    opening = (
+        row
+        + first * jnp.maximum(HW - row, 0)
+        - last * jnp.maximum(row - (clusters - HW - 1), 0)
+    )
+    spots = [columns_v[s : s + 1] - (me * clusters - HW) for s in range(slots)]
+    for w in range(width):
+        found = jnp.full((1, clusters), clusters * slots, jnp.int32)
+        for s in range(slots):
+            found = jnp.where(spots[s] == opening + w, row * slots + s, found)
+        table_v[w : w + 1] = found
+    for s in range(slots):
+        table_v[width + s : width + s + 1] = jnp.clip(spots[s], 0, clusters + 2 * HW - 1)
+    owner = lax.broadcasted_iota(jnp.int32, (1, devices), 1)
+    found = jnp.full((1, devices), -1, jnp.int32)
+    for f in range(far_slots):
+        target = jnp.where(f < count_s[0], targets_s[f], -1)
+        found = jnp.where(owner == target, f, found)
+    far_table_v[0:1] = found
+    tables = [
+        pltpu.make_async_copy(table_v, table_s, table_sem.at[0]),
+        pltpu.make_async_copy(far_table_v, far_table_s, table_sem.at[1]),
+    ]
+    for copy in tables:
+        copy.start()
+
     for copy in inputs[:4]:
         copy.wait()
 
@@ -256,11 +292,13 @@
         halo_copy(False).start()
 
     inputs[5].wait()
+    for copy in tables:
+        copy.wait()
     lh, ll = split(parent[rhs:])
     left_both = jnp.concatenate([lh, ll], axis=0)
 
     def outward(q):
-        f = far_inverse_s[q]
+        f = far_table_s[0, q]
         live = jnp.where(f >= 0, 1.0, 0.0)
         ch, cl = split(coupling_v[jnp.maximum(f, 0)])
         both = nn(left_both, ch)
@@ -297,17 +335,12 @@
     def near_back(i, e0):
         left = masked_left_v[i]
         for w in range(width):
-            s = inverse_s[i * width + w]
-            live = jnp.where(s >= 0, 1.0, 0.0)
-            term = nn(left, near_v[i, jnp.maximum(s, 0)])
-            collected_v[e0 + w] += term * live
+            collected_v[e0 + w] += nn(left, near_v[table_s[w, i]])
 
     def near_forward(i):
-        total = None
-        for s in range(slots):
-            term = nt(ext_v[columns_s[i * slots + s]], near_v[i, s])
-            total = term if total is None else total + term
-        near_out_v[i] = total
+        blocks = jnp.concatenate([near_v[i * slots + s] for s in range(slots)], axis=1)
+        picked = jnp.concatenate([ext_v[table_s[width + s, i]] for s in range(slots)], axis=1)
+        near_out_v[i] = nt(picked, blocks)
 
     for i in range(HW):
         near_back(i, i + first * (HW - i))
@@ -347,11 +380,18 @@
     for i in list(range(HW)) + list(range(clusters - HW, clusters)):
         near_forward(i)
 
-    def middle(i):
-        near_back(i, i)
-        near_forward(i)
-
-    loop(HW, clusters - HW, middle)
+    def middle(g):
+        i = HW + g * HW
+        lefts = [masked_left_v[i + u] for u in range(HW)]
+        for e in range(width + HW - 1):
+            rows = [u for u in range(HW) if 0 <= e - u < width]
+            left = jnp.concatenate([lefts[u] for u in rows], axis=1)
+            blocks = jnp.concatenate([near_v[table_s[e - u, i + u]] for u in rows], axis=0)
+            collected_v[i + e] += nn(left, blocks)
+        for u in range(HW):
+            near_forward(i + u)
+
+    loop(0, (clusters - 2 * HW) // HW, middle)
 
     @pl.when(me > 0)
     def _():
@@ -465,32 +505,17 @@
     clusters, slots = near_columns.shape
     rank, k2 = transfer.shape[1:]
     k3 = slab_transfer.shape[2]
-    far_slots = coupling.shape[1]
     width = 2 * HW + 1
-    me = lax.axis_index(("slab", "leaf"))
-    rows = me * clusters + jnp.arange(clusters, dtype=jnp.int32)
-    start = jnp.clip(rows - HW, 0, devices * clusters - width)
-    wanted = start[:, None] + jnp.arange(width, dtype=jnp.int32)[None, :]
-    number = jnp.arange(1, slots + 1, dtype=jnp.int32)
-    inverse = (
-        jnp.sum(jnp.where(near_columns[:, None, :] == wanted[:, :, None], number, 0), axis=2) - 1
-    )
-    f_index = jnp.arange(far_slots, dtype=jnp.int32)
-    hit = (far_parents[0][None, :] == jnp.arange(devices, dtype=jnp.int32)[:, None]) & (
-        f_index < far_count[0]
-    )[None, :]
-    far_inverse = jnp.sum(jnp.where(hit, f_index + 1, 0), axis=1) - 1
-
     chunk = 2 * rhs // leaves
     smem = pl.BlockSpec(memory_space=pltpu.SMEM)
-    hbm = pl.BlockSpec(memory_space=pl.ANY)
+    hbm = pl.BlockSpec(memory_space=pltpu.HBM)
     vmem = pl.BlockSpec(memory_space=pltpu.VMEM)
     dma = pltpu.SemaphoreType.DMA
     out = jax.ShapeDtypeStruct((rhs, columns), F32)
     return pl.pallas_call(
         functools.partial(kernel, slabs, leaves),
         out_shape=(out, out),
-        in_specs=[smem] * 6 + [hbm] * 8,
+        in_specs=[smem] * 3 + [hbm] * 9,
         out_specs=(vmem, vmem),
         scratch_shapes=[
             pltpu.VMEM((rhs, columns), BF),
@@ -501,7 +526,12 @@
             pltpu.VMEM(coupling.shape[1:], F32),
             pltpu.VMEM((slabs, k3, k3), F32),
             pltpu.VMEM((slabs, k3, k3), F32),
-            pltpu.VMEM(near_blocks.shape, BF),
+            pltpu.VMEM((clusters * slots + 1, B, B), BF),
+            pltpu.VMEM((slots, clusters), jnp.int32),
+            pltpu.VMEM((width + slots, clusters), jnp.int32),
+            pltpu.VMEM((1, devices), jnp.int32),
+            pltpu.SMEM((width + slots, clusters), jnp.int32),
+            pltpu.SMEM((1, devices), jnp.int32),
             pltpu.VMEM((clusters + 2 * HW, rhs, B), BF),
             pltpu.VMEM((clusters, rhs, B), BF),
             pltpu.VMEM((clusters + 2 * HW, rhs, B), F32),
@@ -515,7 +545,8 @@
             pltpu.VMEM((devices, rhs, k2), BF),
             pltpu.VMEM((devices, rhs, k2), BF),
             pltpu.VMEM((2 * rhs, rank), BF),
-            dma((9,)),
+            dma((10,)),
+            dma((2,)),
             dma((2,)),
             dma((2,)),
             dma((2,)),
@@ -530,16 +561,14 @@
             dma((devices,)),
         ],
         compiler_params=pltpu.CompilerParams(
-            collective_id=0, has_side_effects=True, vmem_limit_bytes=48 * 1024 * 1024
+            collective_id=0, has_side_effects=True, vmem_limit_bytes=60 * 1024 * 1024
         ),
         name="h2_step",
     )(
         cluster_points,
-        (near_columns - (me * clusters - HW)).reshape(-1),
-        inverse.reshape(-1),
         far_parents[0],
         far_count,
-        far_inverse,
+        near_columns.T,
         right_sides,
         left_sides,
         leaf_basis,
@@ -547,7 +576,7 @@
         slab_transfer[0],
         coupling[0],
         apex_coupling,
-        near_blocks,
+        near_blocks.reshape(-1, B, B),
     )
 
 

time: 52.8 us -> 44.8 us (0.85)
  local copies, waits for them, and re-layouts: 10.9 us -> 3.74 us
  other arithmetic: 2.25 us -> 0 us
  Pallas kernels: 37.8 us -> 39.4 us
    unnamed x20 -> x2, local copies, waits for them, and re-layouts: 10.5 us -> 3.74 us
    pallas_call x1, Pallas kernels: 37.8 us -> 39.4 us  [shards(): pl.pallas_call(functools.partial(kernel, slabs, leaves), out_shape=(out,...]
    reduce_sum x2 -> x0, other arithmetic: 1.52 us -> none  [the longest x1 0.77 us: shards(): jnp.sum(jnp.where(near_columns[:, None, :] == wanted[:, :, None], number,...]
    sub x3 -> x0, other arithmetic: 0.71 us -> none  [the longest x1 0.69 us: shards(): near_columns - (me * clusters - HW)]
where the time goes in v2:
time: 44.8 us; the launch traced here: 44.4 us
  Pallas kernels  39.4 us (88%)
  local copies, waits for them, and re-layouts  3.74 us (8%)
  between operations  1.29 us (3%)
    pallas_call x1, Pallas kernels, shards(): pl.pallas_call(functools.partial(kernel, slabs, leaves), out_shape=(out,...  39.4 us
    unnamed x2, local copies, waits for them, and re-layouts  3.74 us

profile of v2, /device:TPU:9, one launch (start us, length us, event | category | flops | bytes accessed | tf_op | source)
XLA Modules:
  0.0 44.4 jit_solution(7059537134849729949)
XLA Ops:
  1.3 39.4 %h2_step.1 = (f32[32,4096]{1,0:T(8,128)}, f32[32,4096]{1,0:T(8,128)}) custom-call(s32[32]{0:T(128)} %points_s.1, s32[24]{0:T(128)} %bitcast.9, s32[1]{0:T(128)S(6)} %copy.16.count_s, s32[8,32]{1,0:T(8,128)} %bitcast.8, bf16[32,4096]{1,0:T(8,128)(2,1)} %right_h.1, bf16[32,4096]{1,0:T(8,128)(2,1)} %left_h.1, bf16[32,64,128]{2,1,0:T(8,128)(2,1)} %basis_h.1, ...), custom_call_target="tpu_custom_call" | custom-call | tf_op jit(solution)/shard_map/h2_step/pallas_call | solution.py:515
  40.7 1.9 %copy.17 = f32[32,4096]{1,0:T(8,128)} copy(f32[32,4096]{1,0:T(8,128)} %get-tuple-element.4) | data formatting | bytes 1048576
  42.6 1.9 %copy.18 = f32[32,4096]{1,0:T(8,128)} copy(f32[32,4096]{1,0:T(8,128)} %get-tuple-element.5) | data formatting | bytes 1048576

commit v3 on v2

--- a/solution.py
+++ b/solution.py
@@ -50,8 +50,9 @@
     coupling_h,
     apex_h,
     near_h,
-    product_ref,
-    adjoint_ref,
+    hat_ref,
+    near_h_out,
+    back_h_out,
     right_v,
     left_v,
     basis_v,
@@ -78,7 +79,6 @@
     parents_v,
     outward_v,
     arrived_v,
-    down_v,
     in_sem,
     table_sem,
     halo_send,
@@ -291,6 +291,12 @@
     def _():
         halo_copy(False).start()
 
+    loop(
+        1,
+        devices,
+        lambda k: wide_copy(k, parents_v, parents_v, parent_send, parent_recv, False).start(),
+    )
+
     inputs[5].wait()
     for copy in tables:
         copy.wait()
@@ -319,11 +325,6 @@
     slab_v[me] = total
 
     loop(1, devices, lambda k: wide_copy(k, slab_v, slab_v, slab_send, slab_recv, False).start())
-    loop(
-        1,
-        devices,
-        lambda k: wide_copy(k, parents_v, parents_v, parent_send, parent_recv, False).start(),
-    )
     loop(
         1,
         devices,
@@ -403,6 +404,15 @@
 
     collected_v[HW : 2 * HW] += edge_in_v[1].astype(F32)
     collected_v[clusters : clusters + HW] += edge_in_v[0].astype(F32)
+
+    results = [
+        pltpu.make_async_copy(near_out_v, near_h_out, table_sem.at[0]),
+        pltpu.make_async_copy(
+            collected_v.at[pl.ds(HW, clusters)], back_h_out, table_sem.at[1]
+        ),
+    ]
+    for copy in results:
+        copy.start()
 
     loop(1, devices, lambda k: wide_arrival(k, slab_v, slab_v, slab_send, slab_recv).wait_recv())
     inputs[7].wait()
@@ -442,24 +452,10 @@
         0, devices, lambda d, total: total + arrived_v[d].astype(F32), spread[rhs:]
     )
 
-    hat = jnp.concatenate([far_right, far_left], axis=0)
-    hh, hl = split(hat)
-    hat_both = jnp.concatenate([hh, hl], axis=0)
-
-    def finish(c):
-        th, tl = split(transfer_v[c])
-        both = nt(hat_both, th)
-        down = (both[: 2 * rhs] + both[2 * rhs :] + nt(hh, tl)).astype(BF)
-        out = nn(down, basis_v[c])
-        keep = lane < points_s[c]
-        product_ref[:, window(c)] = jnp.where(keep, near_out_v[c] + out[:rhs], 0.0)
-        adjoint_ref[:, window(c)] = jnp.where(keep, collected_v[c + HW] + out[rhs:], 0.0)
-
-    def finish_group(g):
-        for u in range(unroll):
-            finish(g * unroll + u)
-
-    loop(0, clusters // unroll, finish_group)
+    hat_ref[:rhs] = far_right
+    hat_ref[rhs:] = far_left
+    for copy in results:
+        copy.wait()
 
     loop(1, leaves, lambda k: share_copy(k).wait_send())
     loop(1, devices, lambda k: wide_copy(k, slab_v, slab_v, slab_send, slab_recv, False).wait_send())
@@ -483,6 +479,25 @@
     def _():
         halo_copy(False).wait_send()
         edge_copy(False).wait_send()
+
+
+def finish_kernel(
+    points_s, hat_ref, transfer_ref, basis_ref, near_ref, back_ref, product_ref, adjoint_ref
+):
+    group = transfer_ref.shape[0]
+    rhs = near_ref.shape[1]
+    hh, hl = split(hat_ref[...])
+    hat_both = jnp.concatenate([hh, hl], axis=0)
+    lane = lax.broadcasted_iota(jnp.int32, (rhs, B), 1)
+    for c in range(group):
+        th, tl = split(transfer_ref[c])
+        both = nt(hat_both, th)
+        down = (both[: 2 * rhs] + both[2 * rhs :] + nt(hh, tl)).astype(BF)
+        out = nn(down, basis_ref[c])
+        keep = lane < points_s[pl.program_id(0) * group + c]
+        columns = slice(c * B, (c + 1) * B)
+        product_ref[:, columns] = jnp.where(keep, near_ref[c] + out[:rhs], 0.0)
+        adjoint_ref[:, columns] = jnp.where(keep, back_ref[c] + out[rhs:], 0.0)
 
 
 def shards(
@@ -512,11 +527,12 @@
     vmem = pl.BlockSpec(memory_space=pltpu.VMEM)
     dma = pltpu.SemaphoreType.DMA
     out = jax.ShapeDtypeStruct((rhs, columns), F32)
-    return pl.pallas_call(
+    blocks = jax.ShapeDtypeStruct((clusters, rhs, B), F32)
+    hat, near_out, near_back = pl.pallas_call(
         functools.partial(kernel, slabs, leaves),
-        out_shape=(out, out),
+        out_shape=(jax.ShapeDtypeStruct((2 * rhs, k2), F32), blocks, blocks),
         in_specs=[smem] * 3 + [hbm] * 9,
-        out_specs=(vmem, vmem),
+        out_specs=(vmem, hbm, hbm),
         scratch_shapes=[
             pltpu.VMEM((rhs, columns), BF),
             pltpu.VMEM((rhs, columns), BF),
@@ -544,7 +560,6 @@
             pltpu.VMEM((devices, rhs, k2), BF),
             pltpu.VMEM((devices, rhs, k2), BF),
             pltpu.VMEM((devices, rhs, k2), BF),
-            pltpu.VMEM((2 * rhs, rank), BF),
             dma((10,)),
             dma((2,)),
             dma((2,)),
@@ -578,6 +593,25 @@
         apex_coupling,
         near_blocks.reshape(-1, B, B),
     )
+    group = 8
+    return pl.pallas_call(
+        finish_kernel,
+        out_shape=(out, out),
+        grid=(clusters // group,),
+        in_specs=[
+            smem,
+            pl.BlockSpec((2 * rhs, k2), lambda g: (0, 0)),
+            pl.BlockSpec((group, rank, k2), lambda g: (g, 0, 0)),
+            pl.BlockSpec((group, rank, B), lambda g: (g, 0, 0)),
+            pl.BlockSpec((group, rhs, B), lambda g: (g, 0, 0)),
+            pl.BlockSpec((group, rhs, B), lambda g: (g, 0, 0)),
+        ],
+        out_specs=(
+            pl.BlockSpec((rhs, group * B), lambda g: (0, g)),
+            pl.BlockSpec((rhs, group * B), lambda g: (0, g)),
+        ),
+        name="h2_finish",
+    )(cluster_points, hat, transfer, leaf_basis, near_out, near_back)
 
 
 def solution(mesh):

time: 44.8 us -> 40.2 us (0.90)
  local copies, waits for them, and re-layouts: 3.74 us -> 0 us
  Pallas kernels: 39.4 us -> 38.4 us
    unnamed x2 -> x0, local copies, waits for them, and re-layouts: 3.74 us -> none
    pallas_call x1 -> x2, Pallas kernels: 39.4 us -> 38.4 us  [the longest x1 31 us: shards(): pl.pallas_call(functools.partial(kernel, slabs, leaves), out_shape=(jax.S...]
where the time goes in v3:
time: 40.2 us; the launch traced here: 39.7 us
  Pallas kernels  38.4 us (96%)
  between operations  1.29 us (3%)
    pallas_call x1, Pallas kernels, shards(): pl.pallas_call(functools.partial(kernel, slabs, leaves), out_shape=(jax.S...  31 us
    pallas_call x1, Pallas kernels, shards(): pl.pallas_call(finish_kernel, out_shape=(out, out), grid=(clusters // gro...  7.35 us

profile of v3, /device:TPU:9, one launch (start us, length us, event | category | flops | bytes accessed | tf_op | source)
XLA Modules:
  0.0 39.7 jit_solution(9584614121025513089)
XLA Ops:
  1.3 31.0 %h2_step.1 = (f32[64,128]{1,0:T(8,128)}, f32[32,32,128]{2,1,0:T(8,128)}, f32[32,32,128]{2,1,0:T(8,128)}) custom-call(s32[32]{0:T(128)} %points_s.3, s32[24]{0:T(128)} %bitcast.9, s32[1]{0:T(128)S(6)} %copy.14.count_s, s32[8,32]{1,0:T(8,128)} %bitcast.8, bf16[32,4096]{1,0:T(8,128)(2,1)} %right_h.1, bf16[32,4096]{1,0:T(8,128)(2,1)} %left_h.1, ...), custom_call_target="tpu_custom_call" | custom-call | tf_op jit(solution)/shard_map/h2_step/pallas_call | solution.py:531
  32.3 7.4 %h2_finish.1 = (f32[32,4096]{1,0:T(8,128)}, f32[32,4096]{1,0:T(8,128)}) custom-call(s32[32]{0:T(128)} %points_s.3, f32[64,128]{1,0:T(8,128)} %get-tuple-element.5.hat_ref, f32[32,64,128]{2,1,0:T(8,128)} %transfer_ref.1, bf16[32,64,128]{2,1,0:T(8,128)(2,1)} %basis_ref.1, f32[32,32,128]{2,1,0:T(8,128)} %get-tuple-element.6.near_ref, ...), custom_call_target="tpu_custom_call" | custom-call | tf_op jit(solution)/shard_map/h2_finish/pallas_call | solution.py:597
